TPU v7x, 256 devices: a whole 4x4x8 slice. The times are simulated.
256 devices in a mesh: fsdp: 64 (over x, z, core), rep: 4 (over y).
Axes of the slice: x: 4, y: 4, z: 8, core: 2. Of those that a mesh axis runs over, the one named last changes fastest.
Arguments:
- grad: bfloat16 [128, 256, 2048], P(None, 'fsdp'), may hold values from -6 to 6
- momentum: float32 [128, 256, 2048], P(None, 'fsdp'), may hold values from -6 to 6
- owner_list: int32 [128], replicated, may hold values from 0 to 63, as said below
Outputs:
- new_momentum: float32 [128, 256, 2048], P(None, 'fsdp')
- update: bfloat16 [128, 256, 2048], P(None, 'fsdp')
- owned_update: bfloat16 [256, 256, 2048], P(('fsdp', 'rep'))
Inputs may be any that keep to these rules, and one draw needn't show every extreme that they name: `owner_list`: no owner is named by more than 4 matrices; some owner is named by exactly 4 in every draw.
All inputs are finite; a program needn't handle non-finite values.
Results may differ from a plain program's by a relative error of at most 0.03.
Values may be sent and summed in bfloat16 or wider, within the bound.
A program may use at most 128 MiB of HBM per device.

v0:
```python
import jax
import jax.numpy as jnp
from jax import lax
from jax.sharding import PartitionSpec as P

CAP = 4
ITERS = 5


decay_rate = 0.95
norm_eps = 1e-07
quintic_a = 3.4445
quintic_b = -4.775
quintic_c = 2.0315


def newton(blended):
    values = blended.astype(jnp.float32)
    total = jnp.sqrt(jnp.sum(values * values))
    current = (values / (total + norm_eps)).astype(jnp.bfloat16)
    for iteration in range(ITERS):
        gram = jnp.dot(current, current.T, preferred_element_type=jnp.float32).astype(jnp.bfloat16)
        square = jnp.dot(gram, gram, preferred_element_type=jnp.float32)
        poly = (quintic_b * gram.astype(jnp.float32) + quintic_c * square).astype(jnp.bfloat16)
        applied = jnp.dot(poly, current, preferred_element_type=jnp.float32)
        current = (quintic_a * current.astype(jnp.float32) + applied).astype(jnp.bfloat16)
    return current


def local(grad, momentum, owner_list):
    matrix_count, row_count, col_count = grad.shape
    owner_count = lax.axis_size("fsdp")
    replicas = lax.axis_size("rep")
    capacity = CAP
    per_replica = capacity // replicas
    replica = lax.axis_index("rep")
    new_momentum = decay_rate * momentum + grad.astype(jnp.float32)
    blended = (grad.astype(jnp.float32) + decay_rate * new_momentum).astype(jnp.bfloat16)
    order = jnp.arange(matrix_count)
    earlier = order[None, :] < order[:, None]
    same_owner = owner_list[None, :] == owner_list[:, None]
    slot_index = jnp.sum(jnp.logical_and(earlier, same_owner), axis=1)
    position = slot_index * owner_count + owner_list
    targets = jnp.arange(capacity * owner_count)
    matched = position[None, :] == targets[:, None]
    sources = jnp.sum(jnp.where(matched, order[None, :], 0), axis=1)
    filled = jnp.any(matched, axis=1)
    flattened = blended.reshape(matrix_count, row_count * col_count)
    first_slot = replica * per_replica
    chosen = lax.dynamic_slice_in_dim(sources, first_slot * owner_count, per_replica * owner_count)
    usable = lax.dynamic_slice_in_dim(filled, first_slot * owner_count, per_replica * owner_count)
    picked = jnp.take(flattened, chosen, axis=0)
    picked = jnp.where(usable[:, None], picked, jnp.zeros_like(picked))
    outgoing = picked.reshape(per_replica, owner_count, row_count, col_count)
    received = lax.all_to_all(outgoing, "fsdp", split_axis=1, concat_axis=1, tiled=True)
    items = received.shape[0]
    matrices = received.reshape(items, owner_count * row_count, col_count)
    result = jax.vmap(newton)(matrices)
    finished = result.reshape(items, owner_count, row_count, col_count)
    owned_update = finished.reshape(per_replica, owner_count * row_count, col_count)
    returned = lax.all_to_all(finished, "fsdp", split_axis=1, concat_axis=1, tiled=True)
    complete = lax.all_gather(returned, "rep", axis=0, tiled=True)
    stacked = complete.reshape(capacity * owner_count, row_count, col_count)
    update = jnp.take(stacked, position, axis=0)
    return (new_momentum, update, owned_update)


def solution(mesh):
    in_specs = (P(None, "fsdp", None), P(None, "fsdp", None), P())
    out_specs = (P(None, "fsdp", None), P(None, "fsdp", None), P(("fsdp", "rep"), None, None))
    return jax.shard_map(local, mesh=mesh, in_specs=in_specs, out_specs=out_specs, check_vma=False)
```

profile of v0, /device:TPU:1, one launch (start us, length us, event | category | flops | bytes accessed | tf_op | source)
XLA Modules:
  0.0 174.7 jit_solution(12986220659537661177)
XLA Ops:
  7.2 0.0 all-gather.2.cloned.1.call-start
  7.2 0.9 convert_reduce_fusion
  8.1 0.7 compare_and_fusion.1
  8.8 0.1 select_reduce_fusion
  8.9 0.1 fusion.39
  9.0 5.5 %fusion = (bf16[128,4,2048]{2,1,0:T(4,128)(2,1)S(1)}, f32[128,4,2048]{2,1,0:T(4,128)}) fusion(bf16[128,4,2048]{2,1,0:T(4,128)(2,1)} %param.3, f32[128,4,2048]{2,1,0:T(4,128)} %param.4), kind=kLoop, calls=%fused_computation.4 | loop fusion | flops 6291456 | bytes 12582912 | tf_op jit(solution)/shard_map/convert_element_type | solution.py:38
  14.6 1.4 copy.14
  16.0 0.1 compare_and_fusion
  16.1 1.2 gather_fusion
  17.3 0.8 gather.11
  18.1 0.1 dynamic_slice.6
  18.2 0.7 fusion.18
  18.9 41.3 %all_to_all.10 = bf16[1,64,4,2048]{3,2,0,1:T(4,128)(2,1)S(1)} all-to-all(bf16[1,64,4,2048]{3,2,0,1:T(4,128)(2,1)S(1)} %fusion.18), channel_id=1, replica_groups=mesh['fsdp'=64,'rep'=4] {'fsdp'}, dimensions={1} | all-to-all | bytes 2097152 | tf_op jit(solution)/shard_map/all_to_all | solution.py:55
  60.2 1.7 fusion.6
  62.6 0.6 fusion.7
  63.2 0.3 convert_element_type.146
  63.5 0.5 convolution_convert_fusion.4
  64.0 0.6 fusion.1
  64.6 0.5 convolution_convert_fusion.3
  65.0 0.6 fusion.2
  65.6 0.5 convolution_convert_fusion.2
  66.1 0.6 fusion.3
  66.7 0.5 convolution_convert_fusion.1
  67.1 0.6 fusion.4
  67.7 0.5 convolution_convert_fusion
  68.2 0.6 fusion.5
  68.8 0.0 copy-start
  68.8 0.4 reshape.205
  69.2 34.7 %all_to_all.11 = bf16[1,64,4,2048]{3,2,0,1:T(4,128)(2,1)S(1)} all-to-all(bf16[1,64,4,2048]{3,2,0,1:T(4,128)(2,1)S(1)} %bitcast.39), channel_id=1, replica_groups=mesh['fsdp'=64,'rep'=4] {'fsdp'}, dimensions={1} | all-to-all | bytes 2097152 | tf_op jit(solution)/shard_map/all_to_all | solution.py:61
  104.0 0.0 copy-done
  104.0 1.5 copy.12
  105.5 0.0 all-gather.2.cloned.1.call-update
  105.6 48.0 %all-gather.2.cloned.1.call-done = bf16[4,64,4,2048]{3,1,2,0:T(8,128)(2,1)} async-done(((bf16[1,64,4,2048]{3,1,2,0:T(8,128)(2,1)}), bf16[4,64,4,2048]{3,1,2,0:T(8,128)(2,1)}) %all-gather.2.cloned.1.call-update) | async-done | bytes 4194320 | tf_op jit(solution)/shard_map/all_gather | solution.py:62
  153.5 7.4 %copy.13 = bf16[4,64,4,2048]{3,2,1,0:T(4,128)(2,1)} copy(bf16[4,64,4,2048]{3,1,2,0:T(8,128)(2,1)} %all-gather.2.cloned.1.call-done) | data formatting | bytes 8388608 | tf_op jit(solution)/shard_map/all_gather | solution.py:62
  161.0 4.5 %gather_fusion.1 = bf16[128,4,2048]{2,1,0:T(4,128)(2,1)S(1)} fusion(bf16[256,4,2048]{2,1,0:T(4,128)(2,1)} %bitcast.37, s32[1024]{0:T(1024)S(1)} %pad_clamp_fusion), kind=kCustom, calls=%fused_computation.1 | custom fusion | bytes 4194816 | tf_op jit(solution)/shard_map/jit(_take)/gather | solution.py:64
  165.5 2.4 %broadcast_select_fusion = bf16[128,4,2048]{2,1,0:T(4,128)(2,1)} fusion(bf16[128,4,2048]{2,1,0:T(4,128)(2,1)S(1)} %gather_fusion.1, pred[128]{0:T(512)(128)(4,1)S(1)} %get-tuple-element.3), kind=kLoop, calls=%fused_computation.19 | loop fusion | flops 1048576 | bytes 4194432 | tf_op jit(solution)/shard_map/jit(_take)/select_n | solution.py:64
  (3 shorter events, 0.0 us)
Async XLA Ops:
  7.2 146.4 %all-gather.2.cloned.1.call-start = ((), (), s32[]{:S(2)}) async-start(), calls=%async_computation.2 | async-start | bytes 5242880 | tf_op jit(solution)/shard_map/all_gather | solution.py:62
  68.8 35.2 %copy-start = (bf16[256,2048]{1,0:T(8,128)(2,1)}, bf16[256,2048]{1,0:T(8,128)(2,1)S(1)}, u32[]{:S(2)}) copy-start(bf16[256,2048]{1,0:T(8,128)(2,1)S(1)} %fusion.5) | copy-start | bytes 3145732
Sparse Core Ops, SparseCore 0:
  105.7 47.8 all-gather.1
where the time goes:
time: 175 us
  blocking collectives  76.1 us (43%)
  waiting for transfers between devices  48 us (27%)
  local copies, waits for them, and re-layouts  17.7 us (10%)
  between operations  14.9 us (9%)
  other arithmetic  12.8 us (7%)
  matrix products  5.21 us (3%)
    all_gather x1, waiting for transfers between devices, local(): complete = lax.all_gather(returned, 'rep', axis=0, tiled=True)  48 us
    all_to_all x1, blocking collectives, local(): lax.all_to_all(outgoing, 'fsdp', split_axis=1, concat_axis=1, tiled=True)  41.3 us
    all_to_all x1, blocking collectives, local(): lax.all_to_all(finished, 'fsdp', split_axis=1, concat_axis=1, tiled=True)  34.7 us
    all_gather x1, local copies, waits for them, and re-layouts, local(): complete = lax.all_gather(returned, 'rep', axis=0, tiled=True)  7.43 us
    convert_element_type x1, other arithmetic, local(): (grad.astype(jnp.float32) + decay_rate * new_momentum).astype(jnp.bfloat16)  5.54 us
    gather x1, local copies, waits for them, and re-layouts, local(): update = jnp.take(stacked, position, axis=0)  4.52 us
  transfers between devices with their start and end apart: 1, of which 1 were waited for; matrix products, arithmetic and copies ran while one was open for 0% of the time, Pallas kernels for 0%

commit v1 on v0

v1 whole, which is shorter than its diff:
```python
import functools

import jax
import jax.numpy as jnp
from jax import lax
from jax.experimental import pallas as pl
from jax.experimental.pallas import tpu as pltpu
from jax.sharding import PartitionSpec as P

ITERS = 5
decay_rate = 0.95
norm_eps = 1e-07
quintic_a = 3.4445
quintic_b = -4.775
quintic_c = 2.0315

MESH = pl.DeviceIdType.MESH
NX, NZ, NY = 4, 8, 4
CHIPS = NX * NZ
OWNERS = 2 * CHIPS
MATS = 128


def routing(owner_list, plane, me):
    order = jnp.arange(MATS, dtype=jnp.int32)
    owner = owner_list
    before = order[None, :] < order[:, None]
    slot = jnp.sum(before & (owner[None, :] == owner[:, None]), axis=1, dtype=jnp.int32)
    cell_slot = order // CHIPS
    cell_owner = (order % CHIPS) * 2 + cell_slot // 2
    code = owner * 4 + slot
    cell_code = cell_owner * 4 + cell_slot
    match = code[None, :] == cell_code[:, None]
    filled = jnp.any(match, axis=1)
    in_cell = (slot // 2) == (owner % 2)
    spare_rank = jnp.sum(before & ~in_cell[None, :], axis=1, dtype=jnp.int32)
    empty_rank = jnp.sum(before & ~filled[None, :], axis=1, dtype=jnp.int32)
    stand_in = (spare_rank[None, :] == empty_rank[:, None]) & ~filled[:, None] & ~in_cell[None, :]
    computed = match | stand_in
    cell_of = jnp.sum(jnp.where(computed, order[:, None], 0), axis=0, dtype=jnp.int32)
    chip = jnp.arange(CHIPS, dtype=jnp.int32)
    core = plane // 2
    wanted = cell_of[None, :] == (plane * CHIPS + chip)[:, None]
    to_cells = jnp.sum(jnp.where(wanted, order[None, :], 0), axis=1, dtype=jnp.int32)
    other = code[None, :] == ((chip * 2 + 1 - core) * 4 + plane)[:, None]
    to_others = jnp.sum(jnp.where(other, order[None, :], 0), axis=1, dtype=jnp.int32)
    own = jnp.any(code == me * 4 + plane).astype(jnp.int32)
    return jnp.concatenate([to_cells, to_others, cell_of, own[None]])


def kernel(table, grad_hbm, momentum_hbm, new_ref, update_ref, owned_ref, grad, momentum, staged, x_ref, cells,
           in_sem, send_sem, recv_sem, self_sem, back_send, back_recv, rep_send, rep_recv):
    f = lax.axis_index("fsdp")
    y = lax.axis_index("rep")
    chip = f // 2
    core = f % 2
    px = chip // NZ
    pz = chip % NZ
    cell_core = y // 2
    is_cell = core == cell_core

    load_grad = pltpu.make_async_copy(grad_hbm, grad, in_sem.at[0])
    load_momentum = pltpu.make_async_copy(momentum_hbm, momentum, in_sem.at[1])
    load_grad.start()
    load_momentum.start()

    barrier = pltpu.get_barrier_semaphore()

    @pl.loop(1, OWNERS)
    def _(k):
        pl.semaphore_signal(barrier, inc=1, device_id={"fsdp": lax.rem(f + k, OWNERS)}, device_id_type=MESH)

    for k in range(1, NY):
        pl.semaphore_signal(barrier, inc=1, device_id={"rep": lax.rem(y + k, NY)}, device_id_type=MESH)
    load_grad.wait()
    load_momentum.wait()
    pl.semaphore_wait(barrier, OWNERS - 1 + NY - 1)

    def chip_at(j):
        return lax.rem(px + j // NZ, NX) * NZ + lax.rem(pz + lax.rem(j, NZ), NZ)

    def stage(there, part):
        which = table[part * CHIPS + there]
        g = grad[which].astype(jnp.float32)
        blended = g + decay_rate * (decay_rate * momentum[which] + g)
        staged[part * CHIPS + there] = blended.astype(jnp.bfloat16)

    def send(there, part, to):
        pltpu.make_async_remote_copy(
            src_ref=staged.at[part * CHIPS + there],
            dst_ref=x_ref.at[pl.ds(f * 4, 4)],
            send_sem=send_sem,
            recv_sem=recv_sem,
            device_id={"fsdp": to},
            device_id_type=MESH,
        ).start()

    for part in range(2):
        to_core = cell_core if part == 0 else 1 - cell_core
        stage(chip, part)

        @pl.when(core == to_core)
        def _():
            pltpu.make_async_copy(staged.at[part * CHIPS + chip], x_ref.at[pl.ds(f * 4, 4)], self_sem.at[0]).start()

        @pl.when(core != to_core)
        def _():
            send(chip, part, chip * 2 + to_core)

        @pl.loop(1, CHIPS)
        def _(j):
            there = chip_at(j)
            stage(there, part)
            send(there, part, there * 2 + to_core)

    @pl.loop(0, MATS)
    def _(m):
        new_ref[m] = decay_rate * momentum[m] + grad[m].astype(jnp.float32)

    def receive():
        pltpu.make_async_copy(staged.at[0], x_ref.at[pl.ds(f * 4, 4)], self_sem.at[0]).wait()
        half = staged.at[pl.ds(0, OWNERS - 1)]
        pltpu.make_async_copy(half, half, recv_sem).wait()

    def newton():
        def gram_of(x):
            return lax.dot_general(x, x, (((1,), (1,)), ((), ())), preferred_element_type=jnp.float32)

        def poly_of(gram):
            low = gram.astype(jnp.bfloat16)
            square = jnp.dot(low, low, preferred_element_type=jnp.float32)
            return (quintic_b * low.astype(jnp.float32) + quintic_c * square).astype(jnp.bfloat16)

        def apply(poly, scale):
            for c in range(4):
                cols = pl.ds(c * 512, 512)
                x = x_ref[:, cols]
                applied = jnp.dot(poly, x, preferred_element_type=jnp.float32)
                y_new = quintic_a * x.astype(jnp.float32) + applied
                if scale is not None:
                    y_new = y_new * scale
                x_ref[:, cols] = y_new.astype(jnp.bfloat16)

        gram = gram_of(x_ref[...])
        row = lax.broadcasted_iota(jnp.int32, gram.shape, 0)
        col = lax.broadcasted_iota(jnp.int32, gram.shape, 1)
        total = jnp.sum(jnp.where(row == col, gram, 0.0), axis=(0, 1), keepdims=True)
        scale = 1.0 / (jnp.sqrt(total) + norm_eps)
        apply(poly_of(gram * (scale * scale)), scale)

        @pl.loop(1, ITERS)
        def _(i):
            apply(poly_of(gram_of(x_ref[...])), None)

    def back_arrival(j):
        here = y * CHIPS + lax.rem(px + NX - j // NZ, NX) * NZ + lax.rem(pz + NZ - lax.rem(j, NZ), NZ)
        return here

    @pl.when(is_cell)
    def _():
        receive()
        newton()
        mine = cells.at[y * CHIPS + chip]

        def give_back(j, there, to_core):
            pltpu.make_async_remote_copy(
                src_ref=x_ref.at[pl.ds((there * 2 + to_core) * 4, 4)],
                dst_ref=mine,
                send_sem=back_send,
                recv_sem=back_recv.at[j],
                device_id={"fsdp": there * 2 + to_core},
                device_id_type=MESH,
            ).start()

        pltpu.make_async_copy(x_ref.at[pl.ds(f * 4, 4)], mine, back_recv.at[0]).start()
        give_back(0, chip, 1 - core)

        @pl.loop(1, CHIPS)
        def _(j):
            there = chip_at(j)
            give_back(j, there, 0)
            give_back(j, there, 1)

    @pl.loop(0, CHIPS)
    def _(j):
        here = cells.at[back_arrival(j)]
        pltpu.make_async_copy(here, here, back_recv.at[j]).wait()
        for k in range(1, NY):
            pltpu.make_async_remote_copy(
                src_ref=here,
                dst_ref=here,
                send_sem=rep_send,
                recv_sem=rep_recv.at[k - 1],
                device_id={"rep": lax.rem(y + k, NY)},
                device_id_type=MESH,
            ).start()

    @pl.when(jnp.logical_not(is_cell))
    def _():
        receive()
        newton()

    keep = table[2 * CHIPS + MATS] != 0
    owned_ref[...] = jnp.where(keep, x_ref[...], jnp.zeros(x_ref.shape, x_ref.dtype))

    plane_cells = cells.at[pl.ds(0, CHIPS)]
    for k in range(1, NY):
        pltpu.make_async_copy(plane_cells, plane_cells, rep_recv.at[k - 1]).wait()

    @pl.loop(0, MATS)
    def _(m):
        update_ref[m] = cells[table[2 * CHIPS + m]]

    most = staged.at[pl.ds(0, OWNERS - 1)]
    pltpu.make_async_copy(most, most, send_sem).wait()

    @pl.when(is_cell)
    def _():
        pltpu.make_async_copy(most, most, back_send).wait()

    sent = cells.at[pl.ds(0, 3 * CHIPS)]
    pltpu.make_async_copy(sent, sent, rep_send).wait()


def local(grad, momentum, owner_list):
    mats, rows, cols = grad.shape
    me = lax.axis_index("fsdp")
    table = routing(owner_list, lax.axis_index("rep"), me)
    vmem = pl.BlockSpec(memory_space=pltpu.VMEM)
    hbm = pl.BlockSpec(memory_space=pl.ANY)
    dma = pltpu.SemaphoreType.DMA
    new_momentum, update, owned = pl.pallas_call(
        kernel,
        out_shape=(
            jax.ShapeDtypeStruct(momentum.shape, jnp.float32),
            jax.ShapeDtypeStruct(grad.shape, jnp.bfloat16),
            jax.ShapeDtypeStruct((rows * OWNERS, cols), jnp.bfloat16),
        ),
        in_specs=[pl.BlockSpec(memory_space=pltpu.SMEM), hbm, hbm],
        out_specs=(vmem, vmem, vmem),
        scratch_shapes=[
            pltpu.VMEM((mats, rows, cols), jnp.bfloat16),
            pltpu.VMEM((mats, rows, cols), jnp.float32),
            pltpu.VMEM((OWNERS, rows, cols), jnp.bfloat16),
            pltpu.VMEM((rows * OWNERS, cols), jnp.bfloat16),
            pltpu.VMEM((mats, rows, cols), jnp.bfloat16),
            dma((2,)),
            dma,
            dma,
            dma((1,)),
            dma,
            dma((CHIPS,)),
            dma,
            dma((NY - 1,)),
        ],
        compiler_params=pltpu.CompilerParams(
            collective_id=0, has_side_effects=True, vmem_limit_bytes=40 * 1024 * 1024
        ),
        name="muon",
    )(table, grad, momentum)
    return new_momentum, update, owned[None]


def solution(mesh):
    in_specs = (P(None, "fsdp", None), P(None, "fsdp", None), P())
    out_specs = (P(None, "fsdp", None), P(None, "fsdp", None), P(("fsdp", "rep"), None, None))
    return jax.shard_map(local, mesh=mesh, in_specs=in_specs, out_specs=out_specs, check_vma=False)
```

time: 175 us -> 79.4 us (0.45)
  blocking collectives: 76.1 us -> 0 us
  Pallas kernels: 0 us -> 66.7 us
  waiting for transfers between devices: 48 us -> 0 us
  between operations: 14.9 us -> 1.35 us
  other arithmetic: 12.8 us -> 3.11 us
  local copies, waits for them, and re-layouts: 17.7 us -> 8.09 us
  matrix products: 5.21 us -> 0 us
    all_to_all x2 -> x0, blocking collectives: 76.1 us -> none  [the longest x1 41.3 us: local(): lax.all_to_all(outgoing, 'fsdp', split_axis=1, concat_axis=1, tiled=True)]
    pallas_call x0 -> x1, Pallas kernels: none -> 66.7 us  [local(): pl.pallas_call(kernel, out_shape=(jax.ShapeDtypeStruct(momentum.shape, jn...]
    all_gather x1 -> x0, waiting for transfers between devices: 48 us -> none  [local(): complete = lax.all_gather(returned, 'rep', axis=0, tiled=True)]
    all_gather x1 -> x0, local copies, waits for them, and re-layouts: 7.43 us -> none  [local(): complete = lax.all_gather(returned, 'rep', axis=0, tiled=True)]
    unnamed x3 -> x7, local copies, waits for them, and re-layouts: 1.44 us -> 8.09 us
    gather x3 -> x0, local copies, waits for them, and re-layouts: 6.53 us -> none  [the longest x1 4.52 us: local(): update = jnp.take(stacked, position, axis=0)]
    convert_element_type x2 -> x0, other arithmetic: 6.13 us -> none  [the longest x1 5.54 us: local(): (grad.astype(jnp.float32) + decay_rate * new_momentum).astype(jnp.bfloat16)]
    dot_general x10 -> x0, matrix products: 5.21 us -> none  [the longest x5 2.86 us: newton(): applied = jnp.dot(poly, current, preferred_element_type=jnp.float32)]
  transfers between devices with their start and end apart: 1 -> 0, of which waited for: 1 -> 0; matrix products, arithmetic and copies ran while one was open for 0% -> 0% of each run, Pallas kernels for 0% -> 0%
where the time goes in v1:
time: 79.4 us; the launch traced here: 79.3 us
  Pallas kernels  66.7 us (84%)
  local copies, waits for them, and re-layouts  8.09 us (10%)
  other arithmetic  3.11 us (4%)
  between operations  1.35 us (2%)
    pallas_call x1, Pallas kernels, local(): pl.pallas_call(kernel, out_shape=(jax.ShapeDtypeStruct(momentum.shape, jn...  66.7 us
    unnamed x7, local copies, waits for them, and re-layouts  8.09 us

profile of v1, /device:TPU:1, one launch (start us, length us, event | category | flops | bytes accessed | tf_op | source)
XLA Modules:
  0.0 79.3 jit_solution(17234581013283254870)
XLA Ops:
  0.7 0.9 %convert_reduce_fusion.2 = s32[128]{0:T(128)S(1)} fusion(s32[128]{0:T(128)} %param.5), kind=kLoop, calls=%fused_computation.5 | loop fusion | flops 81792 | bytes 1024 | tf_op jit(solution)/shard_map/reduce_sum | solution.py:28
  1.6 1.3 %compare_reduce_fusion.1 = (pred[]{:T(512)}, s32[128]{0:T(128)S(1)}, pred[128]{0:T(512)(128)(4,1)S(1)}) fusion(s32[]{:T(128)S(6)} %add.87, s32[128]{0:T(128)S(1)} %convert_reduce_fusion.2, s32[128]{0:T(128)} %param.5), kind=kLoop, calls=%fused_computation.14 | loop fusion | flops 4095 | bytes 1669 | tf_op jit(solution)/shard_map/reduce_or | solution.py:47
  3.6 0.2 select_reduce_fusion.1
  3.7 0.2 compare_reduce_fusion
  3.9 0.1 convert_reduce_fusion
  4.0 0.1 select_reduce_fusion
  4.2 0.2 select_reduce_fusion.2
  4.4 0.1 pad_add_fusion.table
  4.5 0.0 copy-start
  4.5 2.2 %copy-done = f32[128,4,2048]{2,1,0:T(4,128)S(1)} copy-done((f32[128,4,2048]{2,1,0:T(4,128)S(1)}, f32[128,4,2048]{2,1,0:T(4,128)}, u32[]{:S(2)}) %copy-start) | copy-done | bytes 4194328
  6.6 0.0 copy-start.1
  6.7 1.6 %copy-done.1 = bf16[128,4,2048]{2,1,0:T(4,128)(2,1)S(1)} copy-done((bf16[128,4,2048]{2,1,0:T(4,128)(2,1)S(1)}, bf16[128,4,2048]{2,1,0:T(4,128)(2,1)}, u32[]{:S(2)}) %copy-start.1) | copy-done | bytes 2097176
  8.2 66.7 %muon.1 = (f32[128,4,2048]{2,1,0:T(4,128)S(1)}, bf16[128,4,2048]{2,1,0:T(4,128)(2,1)S(1)}, bf16[256,2048]{1,0:T(8,128)(2,1)S(1)}) custom-call(s32[193]{0:T(256)S(1)} %pad_add_fusion.table, bf16[128,4,2048]{2,1,0:T(4,128)(2,1)S(1)} %copy-done.1, f32[128,4,2048]{2,1,0:T(4,128)S(1)} %copy-done), custom_call_target="tpu_custom_call" | custom-call | tf_op jit(solution)/shard_map/muon/pallas_call | solution.py:232
  75.0 2.0 %copy.9 = f32[128,4,2048]{2,1,0:T(4,128)} copy(f32[128,4,2048]{2,1,0:T(4,128)S(1)} %get-tuple-element.17) | data formatting | bytes 8388608
  77.0 1.3 %copy.10 = bf16[128,4,2048]{2,1,0:T(4,128)(2,1)} copy(bf16[128,4,2048]{2,1,0:T(4,128)(2,1)S(1)} %get-tuple-element.18) | data formatting | bytes 4194304
  78.3 1.0 %copy.11 = bf16[1,256,2048]{2,1,0:T(8,128)(2,1)} copy(bf16[1,256,2048]{2,1,0:T(8,128)(2,1)S(1)} %bitcast.2) | data formatting | bytes 2097152
  (4 shorter events, 0.0 us)
Async XLA Ops:
  4.5 2.2 %copy-start = (f32[128,4,2048]{2,1,0:T(4,128)S(1)}, f32[128,4,2048]{2,1,0:T(4,128)}, u32[]{:S(2)}) copy-start(f32[128,4,2048]{2,1,0:T(4,128)} %momentum_hbm.1) | copy-start | bytes 12582916
  6.6 1.6 %copy-start.1 = (bf16[128,4,2048]{2,1,0:T(4,128)(2,1)S(1)}, bf16[128,4,2048]{2,1,0:T(4,128)(2,1)}, u32[]{:S(2)}) copy-start(bf16[128,4,2048]{2,1,0:T(4,128)(2,1)} %grad_hbm.1) | copy-start | bytes 6291460

commit v2 on v1

v2 whole, which is shorter than its diff:
```python
import functools

import jax
import jax.numpy as jnp
from jax import lax
from jax.experimental import pallas as pl
from jax.experimental.pallas import tpu as pltpu
from jax.sharding import PartitionSpec as P

ITERS = 5
decay_rate = 0.95
norm_eps = 1e-07
quintic_a = 3.4445
quintic_b = -4.775
quintic_c = 2.0315

MESH = pl.DeviceIdType.MESH
NX, NZ, NY = 4, 8, 4
CHIPS = NX * NZ
OWNERS = 2 * CHIPS
MATS = 128
BLOCK = 4
BLOCKS = CHIPS // BLOCK
LAG = 2
FIRST_STEP = 2


def routing(owner_row, table, plane, me):
    square = (MATS, MATS)
    down = lax.broadcasted_iota(jnp.int32, square, 0)
    along = lax.broadcasted_iota(jnp.int32, square, 1)
    owner_r = jnp.broadcast_to(owner_row, square)
    owner_c = owner_r.T
    same = jnp.where(owner_r == owner_c, 1, 0)
    slot_r = jnp.sum(jnp.where(down < along, same, 0), axis=0, keepdims=True)
    slot_c = jnp.sum(jnp.where(along < down, same, 0), axis=1, keepdims=True)
    code_r = owner_r * 4 + slot_r
    code_c = owner_c * 4 + slot_c

    def cell_code(q):
        slot = q // CHIPS
        return ((q % CHIPS) * 2 + slot // 2) * 4 + slot

    def spare(owner, slot):
        return jnp.where((slot // 2) == (owner % 2), 0, 1)

    spare_r = spare(owner_r, slot_r)
    spare_c = spare(owner_c, slot_c)
    match = jnp.where(code_r == cell_code(down), 1, 0)
    empty_c = 1 - jnp.max(match, axis=1, keepdims=True)
    empty_r = 1 - jnp.max(jnp.where(code_c == cell_code(along), 1, 0), axis=0, keepdims=True)
    spare_rank = jnp.sum(jnp.where(down < along, spare_c, 0), axis=0, keepdims=True)
    empty_rank = jnp.sum(jnp.where(along < down, jnp.broadcast_to(empty_r, square), 0), axis=1, keepdims=True)
    stand_in = jnp.where(spare_rank == empty_rank, spare_r * empty_c, 0)
    cell_of = jnp.sum((match + stand_in) * down, axis=0, keepdims=True)
    cell_of_c = jnp.broadcast_to(cell_of, square).T
    other = ((along - CHIPS) * 2 + 1 - plane // 2) * 4 + plane
    wanted = jnp.where(along < 2 * CHIPS, other, me * 4 + plane)
    hit = jnp.where(along < CHIPS, cell_of_c - plane * CHIPS - along, code_c - wanted) == 0
    number = jnp.where(along < 2 * CHIPS, down, 1)
    table[0:1, :] = jnp.clip(jnp.sum(jnp.where(hit, number, 0), axis=0, keepdims=True), 0, MATS - 1)
    table[1:2, :] = jnp.clip(cell_of, 0, MATS - 1)


def kernel(owner_ref, grad_hbm, momentum_hbm, new_ref, cells, owned_ref, table_ref, grad, momentum, staged, x_ref, table,
           in_sem, send_sem, recv_sem, self_sem, back_send, back_recv, rep_send, up_recv, down_recv, far_recv):
    f = lax.axis_index("fsdp")
    y = lax.axis_index("rep")
    chip = f // 2
    core = f % 2
    px = chip // NZ
    pz = chip % NZ
    cell_core = y // 2
    is_cell = core == cell_core

    load_grad = pltpu.make_async_copy(grad_hbm, grad, in_sem.at[0])
    load_momentum = pltpu.make_async_copy(momentum_hbm, momentum, in_sem.at[1])
    load_grad.start()
    load_momentum.start()

    barrier = pltpu.get_barrier_semaphore()

    @pl.loop(1, OWNERS)
    def _(k):
        pl.semaphore_signal(barrier, inc=1, device_id={"fsdp": lax.rem(f + k, OWNERS)}, device_id_type=MESH)

    for k in range(1, NY):
        pl.semaphore_signal(barrier, inc=1, device_id={"rep": lax.rem(y + k, NY)}, device_id_type=MESH)
    routing(owner_ref[...], table_ref, y, f)
    load_table = pltpu.make_async_copy(table_ref, table, in_sem.at[2])
    load_table.start()
    load_table.wait()
    load_grad.wait()
    load_momentum.wait()
    pl.semaphore_wait(barrier, OWNERS - 1 + NY - 1)

    def chip_at(j):
        return lax.rem(px + j // NZ, NX) * NZ + lax.rem(pz + lax.rem(j, NZ), NZ)

    def stage(there, part):
        which = table[0, part * CHIPS + there]
        g = grad[which].astype(jnp.float32)
        blended = g + decay_rate * (decay_rate * momentum[which] + g)
        staged[part * CHIPS + there] = blended.astype(jnp.bfloat16)

    def send(there, part, to):
        pltpu.make_async_remote_copy(
            src_ref=staged.at[part * CHIPS + there],
            dst_ref=x_ref.at[pl.ds(f * 4, 4)],
            send_sem=send_sem,
            recv_sem=recv_sem,
            device_id={"fsdp": to},
            device_id_type=MESH,
        ).start()

    for part in range(2):
        to_core = cell_core if part == 0 else 1 - cell_core
        stage(chip, part)

        @pl.when(core == to_core)
        def _():
            pltpu.make_async_copy(staged.at[part * CHIPS + chip], x_ref.at[pl.ds(f * 4, 4)], self_sem.at[0]).start()

        @pl.when(core != to_core)
        def _():
            send(chip, part, chip * 2 + to_core)

        @pl.loop(1, CHIPS)
        def _(j):
            there = chip_at(j)
            stage(there, part)
            send(there, part, there * 2 + to_core)

    @pl.loop(0, MATS)
    def _(m):
        new_ref[m] = decay_rate * momentum[m] + grad[m].astype(jnp.float32)

    def receive():
        pltpu.make_async_copy(staged.at[0], x_ref.at[pl.ds(f * 4, 4)], self_sem.at[0]).wait()
        half = staged.at[pl.ds(0, OWNERS - 1)]
        pltpu.make_async_copy(half, half, recv_sem).wait()

    def newton_step(first):
        x = x_ref[...]
        gram = lax.dot_general(x, x, (((1,), (1,)), ((), ())), preferred_element_type=jnp.float32)
        if first:
            row = lax.broadcasted_iota(jnp.int32, gram.shape, 0)
            col = lax.broadcasted_iota(jnp.int32, gram.shape, 1)
            total = jnp.sum(jnp.where(row == col, gram, 0.0), axis=(0, 1), keepdims=True)
            scale = 1.0 / (jnp.sqrt(total) + norm_eps)
            gram = gram * (scale * scale)
        low = gram.astype(jnp.bfloat16)
        square = jnp.dot(low, low, preferred_element_type=jnp.float32)
        poly = (quintic_b * low.astype(jnp.float32) + quintic_c * square).astype(jnp.bfloat16)
        for c in range(4):
            cols = pl.ds(c * 512, 512)
            part = x_ref[:, cols]
            result = quintic_a * part.astype(jnp.float32) + jnp.dot(poly, part, preferred_element_type=jnp.float32)
            if first:
                result = result * scale
            x_ref[:, cols] = result.astype(jnp.bfloat16)

    def back_chip(j):
        return lax.rem(px + NX - j // NZ, NX) * NZ + lax.rem(pz + NZ - lax.rem(j, NZ), NZ)

    up = lax.rem(y + 1, NY)
    below = lax.rem(y + NY - 1, NY)

    @pl.when(is_cell)
    def _():
        receive()
        newton_step(True)

        @pl.loop(1, ITERS)
        def _(i):
            newton_step(False)

        mine = cells.at[y * CHIPS + chip]

        def give_back(j, there, to_core):
            pltpu.make_async_remote_copy(
                src_ref=x_ref.at[pl.ds((there * 2 + to_core) * 4, 4)],
                dst_ref=mine,
                send_sem=back_send,
                recv_sem=back_recv.at[j],
                device_id={"fsdp": there * 2 + to_core},
                device_id_type=MESH,
            ).start()

        pltpu.make_async_copy(x_ref.at[pl.ds(f * 4, 4)], mine, back_recv.at[0]).start()
        give_back(0, chip, 1 - core)

        @pl.loop(1, CHIPS)
        def _(j):
            there = chip_at(j)
            give_back(j, there, 0)
            give_back(j, there, 1)

    def rep_copy(unit, to, sem):
        here = cells.at[unit]
        return pltpu.make_async_remote_copy(
            src_ref=here, dst_ref=here, send_sem=rep_send, recv_sem=sem, device_id={"rep": to}, device_id_type=MESH
        )

    def own(j):
        unit = y * CHIPS + back_chip(j)
        pltpu.make_async_copy(cells.at[unit], cells.at[unit], back_recv.at[j]).wait()
        rep_copy(unit, up, up_recv.at[j]).start()
        rep_copy(unit, below, down_recv.at[j]).start()

    def onward(j):
        unit = below * CHIPS + back_chip(j)
        pltpu.make_async_copy(cells.at[unit], cells.at[unit], up_recv.at[j]).wait()
        rep_copy(unit, up, far_recv).start()
        unit = up * CHIPS + back_chip(j + 1)
        pltpu.make_async_copy(cells.at[unit], cells.at[unit], down_recv.at[j + 1]).wait()
        rep_copy(unit, below, far_recv).start()

    @pl.loop(0, BLOCKS + LAG)
    def _(b):
        @pl.when(b < BLOCKS)
        def _():
            @pl.loop(0, BLOCK)
            def _(i):
                own(b * BLOCK + i)

        @pl.when(b >= LAG)
        def _():
            @pl.loop(0, BLOCK // 2)
            def _(i):
                onward((b - LAG) * BLOCK + 2 * i)

        step = b - FIRST_STEP

        @pl.when(jnp.logical_and(jnp.logical_not(is_cell), step == 0))
        def _():
            receive()
            newton_step(True)

        @pl.when(jnp.logical_and(jnp.logical_not(is_cell), jnp.logical_and(step > 0, step < ITERS)))
        def _():
            newton_step(False)

    keep = table[0, 2 * CHIPS] != 0
    owned_ref[...] = jnp.where(keep, x_ref[...], jnp.zeros(x_ref.shape, x_ref.dtype))

    @pl.loop(0, CHIPS // 2)
    def _(i):
        unit = cells.at[0]
        pltpu.make_async_copy(unit, unit, up_recv.at[2 * i + 1]).wait()
        pltpu.make_async_copy(unit, unit, down_recv.at[2 * i]).wait()

    plane_cells = cells.at[pl.ds(0, CHIPS)]
    pltpu.make_async_copy(plane_cells, plane_cells, far_recv).wait()

    most = staged.at[pl.ds(0, OWNERS - 1)]
    pltpu.make_async_copy(most, most, send_sem).wait()

    @pl.when(is_cell)
    def _():
        pltpu.make_async_copy(most, most, back_send).wait()

    sent = cells.at[pl.ds(0, 3 * CHIPS)]
    pltpu.make_async_copy(sent, sent, rep_send).wait()


def finish(table, new_ref, cells, owned_ref, new_out, update_out, owned_out, sem):
    new_copy = pltpu.make_async_copy(new_ref, new_out, sem.at[0])
    owned_copy = pltpu.make_async_copy(owned_ref, owned_out, sem.at[1])
    new_copy.start()

    @pl.loop(0, MATS, unroll=8)
    def _(m):
        pltpu.make_async_copy(cells.at[table[1, m]], update_out.at[m], sem.at[2]).start()

    owned_copy.start()
    pltpu.make_async_copy(cells, update_out, sem.at[2]).wait()
    new_copy.wait()
    owned_copy.wait()


def local(grad, momentum, owner_list):
    mats, rows, cols = grad.shape
    vmem = pl.BlockSpec(memory_space=pltpu.VMEM)
    smem = pl.BlockSpec(memory_space=pltpu.SMEM)
    hbm = pl.BlockSpec(memory_space=pltpu.HBM)
    pin = pltpu.with_memory_space_constraint
    hold = pl.BlockSpec(memory_space=pl.ANY)
    dma = pltpu.SemaphoreType.DMA
    outs = (
        jax.ShapeDtypeStruct(momentum.shape, jnp.float32),
        jax.ShapeDtypeStruct(grad.shape, jnp.bfloat16),
        jax.ShapeDtypeStruct((rows * OWNERS, cols), jnp.bfloat16),
    )
    new_momentum, cells, owned, table = pl.pallas_call(
        kernel,
        out_shape=(*(pltpu.VMEM(o.shape, o.dtype) for o in outs), pltpu.VMEM((2, MATS), jnp.int32)),
        in_specs=[vmem, hbm, hbm],
        out_specs=(vmem, vmem, vmem, vmem),
        scratch_shapes=[
            pltpu.VMEM((mats, rows, cols), jnp.bfloat16),
            pltpu.VMEM((mats, rows, cols), jnp.float32),
            pltpu.VMEM((OWNERS, rows, cols), jnp.bfloat16),
            pltpu.VMEM((rows * OWNERS, cols), jnp.bfloat16),
            pltpu.SMEM((2, MATS), jnp.int32),
            dma((3,)),
            dma,
            dma,
            dma((1,)),
            dma,
            dma((CHIPS,)),
            dma,
            dma((CHIPS,)),
            dma((CHIPS,)),
            dma,
        ],
        compiler_params=pltpu.CompilerParams(
            collective_id=0, has_side_effects=True, vmem_limit_bytes=40 * 1024 * 1024
        ),
        name="muon",
    )(owner_list.reshape(1, MATS), pin(grad, pltpu.HBM), pin(momentum, pltpu.HBM))
    new_momentum, update, owned = pl.pallas_call(
        finish,
        out_shape=outs,
        in_specs=[smem, hold, hold, hold],
        out_specs=(hbm, hbm, hbm),
        scratch_shapes=[dma((3,))],
        compiler_params=pltpu.CompilerParams(vmem_limit_bytes=1024 * 1024),
        name="finish",
    )(table, new_momentum, cells, owned)
    return new_momentum, update, owned[None]


def solution(mesh):
    in_specs = (P(None, "fsdp", None), P(None, "fsdp", None), P())
    out_specs = (P(None, "fsdp", None), P(None, "fsdp", None), P(("fsdp", "rep"), None, None))
    return jax.shard_map(local, mesh=mesh, in_specs=in_specs, out_specs=out_specs, check_vma=False)
```

time: 79.4 us -> 66.9 us (0.84)
  local copies, waits for them, and re-layouts: 8.09 us -> 0.65 us
  other arithmetic: 3.11 us -> 0 us
  Pallas kernels: 66.7 us -> 65.5 us
    unnamed x7 -> x2, local copies, waits for them, and re-layouts: 8.09 us -> 0.65 us
    reduce_sum x5 -> x0, other arithmetic: 1.51 us -> none  [the longest x1 0.9 us: routing(): jnp.sum(before & (owner[None, :] == owner[:, None]), axis=1, dtype=jnp.in...]
    reduce_or x2 -> x0, other arithmetic: 1.48 us -> none  [the longest x1 1.31 us: routing(): own = jnp.any(code == me * 4 + plane).astype(jnp.int32)]
    pallas_call x1 -> x2, Pallas kernels: 66.7 us -> 65.5 us  [the longest x1 62 us: local(): pl.pallas_call(kernel, out_shape=(*(pltpu.VMEM(o.shape, o.dtype) for o in...]
where the time goes in v2:
time: 66.9 us; the launch traced here: 66.8 us
  Pallas kernels  65.5 us (98%)
    pallas_call x1, Pallas kernels, local(): pl.pallas_call(kernel, out_shape=(*(pltpu.VMEM(o.shape, o.dtype) for o in...  62 us
    pallas_call x1, Pallas kernels, local(): pl.pallas_call(finish, out_shape=outs, in_specs=[smem, hold, hold, hold],...  3.53 us

profile of v2, /device:TPU:1, one launch (start us, length us, event | category | flops | bytes accessed | tf_op | source)
XLA Modules:
  0.0 66.8 jit_solution(2217942921664525938)
XLA Ops:
  0.6 0.0 copy-start
  0.6 0.6 copy-done
  1.3 62.0 %muon.1 = (f32[128,4,2048]{2,1,0:T(4,128)S(1)}, bf16[128,4,2048]{2,1,0:T(4,128)(2,1)S(1)}, bf16[256,2048]{1,0:T(8,128)(2,1)S(1)}, s32[2,128]{1,0:T(2,128)S(1)}) custom-call(s32[1,128]{1,0:T(1,128)S(1)} %bitcast.2, bf16[128,4,2048]{2,1,0:T(4,128)(2,1)} %grad_hbm.1, f32[128,4,2048]{2,1,0:T(4,128)} %momentum_hbm.1), custom_call_target="tpu_custom_call" | custom-call | tf_op jit(solution)/shard_map/muon/pallas_call | solution.py:295
  63.3 3.5 %finish.1 = (f32[128,4,2048]{2,1,0:T(4,128)}, bf16[128,4,2048]{2,1,0:T(4,128)(2,1)}, bf16[256,2048]{1,0:T(8,128)(2,1)}) custom-call(s32[2,128]{1,0:T(2,128)S(1)} %get-tuple-element.10.table, f32[128,4,2048]{2,1,0:T(4,128)S(1)} %get-tuple-element.11.new_ref, bf16[128,4,2048]{2,1,0:T(4,128)(2,1)S(1)} %get-tuple-element.12.cells, ...), custom_call_target="tpu_custom_call" | custom-call | tf_op jit(solution)/shard_map/finish/pallas_call | solution.py:322
Async XLA Ops:
  0.6 0.7 copy-start

commit v3 on v2

v3 whole, which is shorter than its diff:
```python
import functools

import jax
import jax.numpy as jnp
from jax import lax
from jax.experimental import pallas as pl
from jax.experimental.pallas import tpu as pltpu
from jax.sharding import PartitionSpec as P

ITERS = 5
decay_rate = 0.95
norm_eps = 1e-07
quintic_a = 3.4445
quintic_b = -4.775
quintic_c = 2.0315

MESH = pl.DeviceIdType.MESH
NX, NZ, NY = 4, 8, 4
CHIPS = NX * NZ
OWNERS = 2 * CHIPS
MATS = 128
HALF = CHIPS // 2
BLOCK = 4
BLOCKS = CHIPS // BLOCK
LAG = 2
ORDER = (0, 1, 4, 2, 5, 3, 6, 7)
STEP_AT = (7, 8, 9, 9, 9)
WIDTH = 256


def routing(owner_row, table, plane, me, px, pz):
    square = (MATS, MATS)
    down = lax.broadcasted_iota(jnp.int32, square, 0)
    along = lax.broadcasted_iota(jnp.int32, square, 1)
    owner_r = jnp.broadcast_to(owner_row, square)
    owner_c = owner_r.T
    same = jnp.where(owner_r == owner_c, 1, 0)
    slot_r = jnp.sum(jnp.where(down < along, same, 0), axis=0, keepdims=True)
    slot_c = jnp.sum(jnp.where(along < down, same, 0), axis=1, keepdims=True)
    code_r = owner_r * 4 + slot_r
    code_c = owner_c * 4 + slot_c

    def cell_code(q):
        slot = q // CHIPS
        return ((q % CHIPS) * 2 + slot // 2) * 4 + slot

    def spare(owner, slot):
        return jnp.where((slot // 2) == (owner % 2), 0, 1)

    spare_r = spare(owner_r, slot_r)
    spare_c = spare(owner_c, slot_c)
    match = jnp.where(code_r == cell_code(down), 1, 0)
    empty_c = 1 - jnp.max(match, axis=1, keepdims=True)
    empty_r = 1 - jnp.max(jnp.where(code_c == cell_code(along), 1, 0), axis=0, keepdims=True)
    spare_rank = jnp.sum(jnp.where(down < along, spare_c, 0), axis=0, keepdims=True)
    empty_rank = jnp.sum(jnp.where(along < down, jnp.broadcast_to(empty_r, square), 0), axis=1, keepdims=True)
    stand_in = jnp.where(spare_rank == empty_rank, spare_r * empty_c, 0)
    cell_of = jnp.sum((match + stand_in) * down, axis=0, keepdims=True)
    cell_of_c = jnp.broadcast_to(cell_of, square).T
    other = ((along - CHIPS) * 2 + 1 - plane // 2) * 4 + plane
    wanted = jnp.where(along < 2 * CHIPS, other, me * 4 + plane)
    hit = jnp.where(along < CHIPS, cell_of_c - plane * CHIPS - along, code_c - wanted) == 0
    number = jnp.where(along < 2 * CHIPS, down, 1)
    table[0:1, :] = jnp.clip(jnp.sum(jnp.where(hit, number, 0), axis=0, keepdims=True), 0, MATS - 1)
    chip = down % CHIPS
    x, z = chip // NZ, chip % NZ
    place = (down // CHIPS) * CHIPS + (x + z) % 2 * HALF + (px + NX - x) % NX * BLOCK + (pz + NZ - z) % NZ // 2
    place = jnp.sum((match + stand_in) * place, axis=0, keepdims=True)
    table[1:2, :] = jnp.clip(place, 0, MATS - 1)


def kernel(owner_hbm, grad_hbm, momentum_hbm, new_ref, cells, owned_ref, table_ref, owner, grad, momentum, staged, x_ref,
           gram_ref, table, in_sem, send_sem, recv_sem, self_sem, back_send, back_recv, rep_send, up_recv, down_recv,
           far_recv):
    f = lax.axis_index("fsdp")
    y = lax.axis_index("rep")
    chip = f // 2
    core = f % 2
    px = chip // NZ
    pz = chip % NZ
    parity = lax.rem(px + pz, 2)
    cell_core = y // 2
    is_cell = core == cell_core
    no_cell = jnp.logical_not(is_cell)

    load_owner = pltpu.make_async_copy(owner_hbm, owner, in_sem.at[3])
    load_grad = pltpu.make_async_copy(grad_hbm, grad, in_sem.at[0])
    load_momentum = pltpu.make_async_copy(momentum_hbm, momentum, in_sem.at[1])
    load_owner.start()
    load_grad.start()
    load_momentum.start()

    barrier = pltpu.get_barrier_semaphore()

    @pl.loop(1, OWNERS)
    def _(k):
        pl.semaphore_signal(barrier, inc=1, device_id={"fsdp": lax.rem(f + k, OWNERS)}, device_id_type=MESH)

    for k in range(1, NY):
        pl.semaphore_signal(barrier, inc=1, device_id={"rep": lax.rem(y + k, NY)}, device_id_type=MESH)
    load_owner.wait()
    routing(owner[...], table_ref, y, f, px, pz)
    load_table = pltpu.make_async_copy(table_ref, table, in_sem.at[2])
    load_table.start()
    load_table.wait()
    load_grad.wait()
    load_momentum.wait()
    pl.semaphore_wait(barrier, OWNERS - 1 + NY - 1)

    def stage(there, part):
        which = table[0, part * CHIPS + there]
        g = grad[which].astype(jnp.float32)
        blended = g + decay_rate * (decay_rate * momentum[which] + g)
        staged[part * CHIPS + there] = blended.astype(jnp.bfloat16)

    def send(there, part, to):
        rows = staged.at[part * CHIPS + there]
        target = x_ref.at[pl.ds(f * 4, 4)]

        @pl.when(to == f)
        def _():
            pltpu.make_async_copy(rows, target, self_sem.at[0]).start()

        @pl.when(to != f)
        def _():
            pltpu.make_async_remote_copy(
                src_ref=rows,
                dst_ref=target,
                send_sem=send_sem,
                recv_sem=recv_sem,
                device_id={"fsdp": to},
                device_id_type=MESH,
            ).start()

    def each(batch, action):
        @pl.loop(0, HALF)
        def _(i):
            dx = i // 4
            dz = 2 * lax.rem(i, 4) + lax.rem(dx + parity + batch, 2)
            action(lax.rem(px + dx, NX) * NZ + lax.rem(pz + dz, NZ))

    def forward(there):
        stage(there, 0)
        send(there, 0, there * 2 + cell_core)

    def other(there):
        stage(there, 1)
        send(there, 1, there * 2 + 1 - cell_core)

    for batch in range(2):
        each(batch, forward)

    @pl.when(no_cell)
    def _():
        for batch in range(2):
            each(batch, other)

    @pl.loop(0, MATS)
    def _(m):
        new_ref[m] = decay_rate * momentum[m] + grad[m].astype(jnp.float32)

    def receive():
        pltpu.make_async_copy(staged.at[0], x_ref.at[pl.ds(f * 4, 4)], self_sem.at[0]).wait()
        half = staged.at[pl.ds(0, OWNERS - 1)]
        pltpu.make_async_copy(half, half, recv_sem).wait()

    def gram_of(x):
        return lax.dot_general(x, x, (((1,), (1,)), ((), ())), preferred_element_type=jnp.float32)

    def newton_step(first, last):
        if first:
            gram = gram_of(x_ref[...])
            row = lax.broadcasted_iota(jnp.int32, gram.shape, 0)
            col = lax.broadcasted_iota(jnp.int32, gram.shape, 1)
            total = jnp.sum(jnp.where(row == col, gram, 0.0), axis=(0, 1), keepdims=True)
            scale = 1.0 / (jnp.sqrt(total) + norm_eps)
            gram = gram * (scale * scale)
        else:
            gram = gram_ref[...]
        low = gram.astype(jnp.bfloat16)
        square = jnp.dot(low, low, preferred_element_type=jnp.float32)
        poly = (quintic_b * low.astype(jnp.float32) + quintic_c * square).astype(jnp.bfloat16)
        gram = None
        for c in range(x_ref.shape[1] // WIDTH):
            cols = pl.ds(c * WIDTH, WIDTH)
            x = x_ref[:, cols]
            result = quintic_a * x.astype(jnp.float32) + jnp.dot(poly, x, preferred_element_type=jnp.float32)
            if first:
                result = result * scale
            result = result.astype(jnp.bfloat16)
            x_ref[:, cols] = result
            if not last:
                gram = gram_of(result) if gram is None else gram + gram_of(result)
        if not last:
            gram_ref[...] = gram

    @pl.when(is_cell)
    def _():
        receive()
        for step in range(ITERS):
            newton_step(step == 0, step == ITERS - 1)
        base = y * CHIPS + parity * HALF

        @pl.loop(0, CHIPS)
        def _(j):
            dx = j // NZ
            dz = lax.rem(j, NZ)
            there = lax.rem(px + dx, NX) * NZ + lax.rem(pz + dz, NZ)
            target = cells.at[base + dx * BLOCK + dz // 2]
            arrived = back_recv.at[parity * NX + dx]
            for to_core in range(2):
                to = there * 2 + to_core
                rows = x_ref.at[pl.ds(to * 4, 4)]

                @pl.when(to == f)
                def _():
                    pltpu.make_async_copy(rows, target, arrived).start()

                @pl.when(to != f)
                def _():
                    pltpu.make_async_remote_copy(
                        src_ref=rows,
                        dst_ref=target,
                        send_sem=back_send,
                        recv_sem=arrived,
                        device_id={"fsdp": to},
                        device_id_type=MESH,
                    ).start()

        for batch in range(2):
            each(batch, other)

    up = lax.rem(y + 1, NY)
    below = lax.rem(y + NY - 1, NY)

    def block_of(plane, b):
        return cells.at[pl.ds(plane * CHIPS + b * BLOCK, BLOCK)]

    def arrive(plane, b, sem):
        pltpu.make_async_copy(block_of(plane, b), block_of(plane, b), sem).wait()

    def pass_on(plane, b, to, sem):
        pltpu.make_async_remote_copy(
            src_ref=block_of(plane, b),
            dst_ref=block_of(plane, b),
            send_sem=rep_send,
            recv_sem=sem,
            device_id={"rep": to},
            device_id_type=MESH,
        ).start()

    for at in range(BLOCKS + LAG):
        if at < BLOCKS:
            b = ORDER[at]
            arrive(y, b, back_recv.at[b])
            pass_on(y, b, up, up_recv.at[b])
            pass_on(y, b, below, down_recv.at[b])
        if at >= LAG:
            b = ORDER[at - LAG]
            if b % 2 == 0:
                arrive(below, b, up_recv.at[b])
                pass_on(below, b, up, far_recv)
            else:
                arrive(up, b, down_recv.at[b])
                pass_on(up, b, below, far_recv)
        for step in range(ITERS):
            if STEP_AT[step] == at:

                @pl.when(no_cell)
                def _():
                    if step == 0:
                        receive()
                    newton_step(step == 0, step == ITERS - 1)

    keep = table[0, 2 * CHIPS] != 0
    owned_ref[...] = jnp.where(keep, x_ref[...], jnp.zeros(x_ref.shape, x_ref.dtype))

    for b in range(0, BLOCKS, 2):
        arrive(up, b, down_recv.at[b])
        arrive(below, b + 1, up_recv.at[b + 1])
    plane_cells = cells.at[pl.ds(0, CHIPS)]
    pltpu.make_async_copy(plane_cells, plane_cells, far_recv).wait()

    most = staged.at[pl.ds(0, OWNERS - 1)]
    pltpu.make_async_copy(most, most, send_sem).wait()

    @pl.when(is_cell)
    def _():
        pltpu.make_async_copy(most, most, back_send).wait()

    sent = cells.at[pl.ds(0, 3 * CHIPS)]
    pltpu.make_async_copy(sent, sent, rep_send).wait()


def finish(table, new_ref, cells, owned_ref, new_out, update_out, owned_out, sem):
    new_copy = pltpu.make_async_copy(new_ref, new_out, sem.at[0])
    owned_copy = pltpu.make_async_copy(owned_ref, owned_out, sem.at[1])
    new_copy.start()

    @pl.loop(0, MATS, unroll=8)
    def _(m):
        pltpu.make_async_copy(cells.at[table[1, m]], update_out.at[m], sem.at[2]).start()

    owned_copy.start()
    pltpu.make_async_copy(cells, update_out, sem.at[2]).wait()
    new_copy.wait()
    owned_copy.wait()


def local(grad, momentum, owner_list):
    mats, rows, cols = grad.shape
    vmem = pl.BlockSpec(memory_space=pltpu.VMEM)
    smem = pl.BlockSpec(memory_space=pltpu.SMEM)
    hbm = pl.BlockSpec(memory_space=pltpu.HBM)
    pin = pltpu.with_memory_space_constraint
    hold = pl.BlockSpec(memory_space=pl.ANY)
    dma = pltpu.SemaphoreType.DMA
    outs = (
        jax.ShapeDtypeStruct(momentum.shape, jnp.float32),
        jax.ShapeDtypeStruct(grad.shape, jnp.bfloat16),
        jax.ShapeDtypeStruct((rows * OWNERS, cols), jnp.bfloat16),
    )
    new_momentum, cells, owned, table = pl.pallas_call(
        kernel,
        out_shape=(*(pltpu.VMEM(o.shape, o.dtype) for o in outs), pltpu.VMEM((2, MATS), jnp.int32)),
        in_specs=[hbm, hbm, hbm],
        out_specs=(vmem, vmem, vmem, vmem),
        scratch_shapes=[
            pltpu.VMEM((1, MATS), jnp.int32),
            pltpu.VMEM((mats, rows, cols), jnp.bfloat16),
            pltpu.VMEM((mats, rows, cols), jnp.float32),
            pltpu.VMEM((OWNERS, rows, cols), jnp.bfloat16),
            pltpu.VMEM((rows * OWNERS, cols), jnp.bfloat16),
            pltpu.VMEM((rows * OWNERS, rows * OWNERS), jnp.float32),
            pltpu.SMEM((2, MATS), jnp.int32),
            dma((4,)),
            dma,
            dma,
            dma((1,)),
            dma,
            dma((BLOCKS,)),
            dma,
            dma((BLOCKS,)),
            dma((BLOCKS,)),
            dma,
        ],
        compiler_params=pltpu.CompilerParams(
            collective_id=0, has_side_effects=True, vmem_limit_bytes=40 * 1024 * 1024
        ),
        name="muon",
    )(pin(owner_list.reshape(1, MATS), pltpu.HBM), pin(grad, pltpu.HBM), pin(momentum, pltpu.HBM))
    new_momentum, update, owned = pl.pallas_call(
        finish,
        out_shape=outs,
        in_specs=[smem, hold, hold, hold],
        out_specs=(hbm, hbm, hbm),
        scratch_shapes=[dma((3,))],
        compiler_params=pltpu.CompilerParams(vmem_limit_bytes=1024 * 1024),
        name="finish",
    )(table, new_momentum, cells, owned)
    return new_momentum, update, owned[None]


def solution(mesh):
    in_specs = (P(None, "fsdp", None), P(None, "fsdp", None), P())
    out_specs = (P(None, "fsdp", None), P(None, "fsdp", None), P(("fsdp", "rep"), None, None))
    return jax.shard_map(local, mesh=mesh, in_specs=in_specs, out_specs=out_specs, check_vma=False)
```

time: 66.9 us -> 62 us (0.927)
  Pallas kernels: 65.5 us -> 61.3 us
    pallas_call x1, Pallas kernels: 62 us -> 57.7 us  [local(): pl.pallas_call(kernel, out_shape=(*(pltpu.VMEM(o.shape, o.dtype) for o in...]
where the time goes in v3:
time: 62 us; the launch traced here: 61.9 us
  Pallas kernels  61.3 us (99%)
  between operations  0.64 us (1%)
    pallas_call x1, Pallas kernels, local(): pl.pallas_call(kernel, out_shape=(*(pltpu.VMEM(o.shape, o.dtype) for o in...  57.7 us
    pallas_call x1, Pallas kernels, local(): pl.pallas_call(finish, out_shape=outs, in_specs=[smem, hold, hold, hold],...  3.53 us

profile of v3, /device:TPU:1, one launch (start us, length us, event | category | flops | bytes accessed | tf_op | source)
XLA Modules:
  0.0 61.9 jit_solution(8824502993998065454)
XLA Ops:
  0.6 57.7 %muon.1 = (f32[128,4,2048]{2,1,0:T(4,128)S(1)}, bf16[128,4,2048]{2,1,0:T(4,128)(2,1)S(1)}, bf16[256,2048]{1,0:T(8,128)(2,1)S(1)}, s32[2,128]{1,0:T(2,128)S(1)}) custom-call(s32[1,128]{1,0:T(1,128)} %bitcast.2, bf16[128,4,2048]{2,1,0:T(4,128)(2,1)} %grad_hbm.1, f32[128,4,2048]{2,1,0:T(4,128)} %momentum_hbm.1), custom_call_target="tpu_custom_call" | custom-call | tf_op jit(solution)/shard_map/muon/pallas_call | solution.py:323
  58.4 3.5 %finish.1 = (f32[128,4,2048]{2,1,0:T(4,128)}, bf16[128,4,2048]{2,1,0:T(4,128)(2,1)}, bf16[256,2048]{1,0:T(8,128)(2,1)}) custom-call(s32[2,128]{1,0:T(2,128)S(1)} %get-tuple-element.10.table, f32[128,4,2048]{2,1,0:T(4,128)S(1)} %get-tuple-element.11.new_ref, bf16[128,4,2048]{2,1,0:T(4,128)(2,1)S(1)} %get-tuple-element.12.cells, ...), custom_call_target="tpu_custom_call" | custom-call | tf_op jit(solution)/shard_map/finish/pallas_call | solution.py:352

commit v4 on v3

--- a/solution.py
+++ b/solution.py
@@ -22,9 +22,9 @@
 HALF = CHIPS // 2
 BLOCK = 4
 BLOCKS = CHIPS // BLOCK
-LAG = 2
+LAG = 1
 ORDER = (0, 1, 4, 2, 5, 3, 6, 7)
-STEP_AT = (7, 8, 9, 9, 9)
+STEP_AT = (7, 8, 8, 8, 8)
 WIDTH = 256
 
 
@@ -92,7 +92,7 @@
 
     barrier = pltpu.get_barrier_semaphore()
 
-    @pl.loop(1, OWNERS)
+    @pl.loop(1, OWNERS, unroll=21)
     def _(k):
         pl.semaphore_signal(barrier, inc=1, device_id={"fsdp": lax.rem(f + k, OWNERS)}, device_id_type=MESH)
 

time: 62 us -> 62.7 us (1.011)
    pallas_call x1, Pallas kernels: 57.7 us -> 58.4 us  [local(): pl.pallas_call(kernel, out_shape=(*(pltpu.VMEM(o.shape, o.dtype) for o in...]
where the time goes in v4:
time: 62.7 us; the launch traced here: 62.6 us
  Pallas kernels  61.9 us (99%)
  between operations  0.64 us (1%)
    pallas_call x1, Pallas kernels, local(): pl.pallas_call(kernel, out_shape=(*(pltpu.VMEM(o.shape, o.dtype) for o in...  58.4 us
    pallas_call x1, Pallas kernels, local(): pl.pallas_call(finish, out_shape=outs, in_specs=[smem, hold, hold, hold],...  3.53 us

profile of v4, /device:TPU:1, one launch (start us, length us, event | category | flops | bytes accessed | tf_op | source)
XLA Modules:
  0.0 62.6 jit_solution(15301844855250801693)
XLA Ops:
  0.6 58.4 %muon.1 = (f32[128,4,2048]{2,1,0:T(4,128)S(1)}, bf16[128,4,2048]{2,1,0:T(4,128)(2,1)S(1)}, bf16[256,2048]{1,0:T(8,128)(2,1)S(1)}, s32[2,128]{1,0:T(2,128)S(1)}) custom-call(s32[1,128]{1,0:T(1,128)} %bitcast.2, bf16[128,4,2048]{2,1,0:T(4,128)(2,1)} %grad_hbm.1, f32[128,4,2048]{2,1,0:T(4,128)} %momentum_hbm.1), custom_call_target="tpu_custom_call" | custom-call | tf_op jit(solution)/shard_map/muon/pallas_call | solution.py:323
  59.1 3.5 %finish.1 = (f32[128,4,2048]{2,1,0:T(4,128)}, bf16[128,4,2048]{2,1,0:T(4,128)(2,1)}, bf16[256,2048]{1,0:T(8,128)(2,1)}) custom-call(s32[2,128]{1,0:T(2,128)S(1)} %get-tuple-element.10.table, f32[128,4,2048]{2,1,0:T(4,128)S(1)} %get-tuple-element.11.new_ref, bf16[128,4,2048]{2,1,0:T(4,128)(2,1)S(1)} %get-tuple-element.12.cells, ...), custom_call_target="tpu_custom_call" | custom-call | tf_op jit(solution)/shard_map/finish/pallas_call | solution.py:352
